TPU v7x, 256 devices: a whole 4x4x8 slice. The times are simulated.
256 devices in a mesh: bubble: 16 (over y_hi, z), panel: 16 (over y_lo, x, core).
Axes of the slice: x: 4, y: 4 (y_hi: 2, y_lo: 2; y = y_hi * 2 + y_lo), z: 8, core: 2. Of those that a mesh axis runs over, the one named last changes fastest.
Arguments:
- density: float32 [128, 12288], P('bubble', 'panel'), may hold values from -6 to 6
- right_side: float32 [128, 12288], P('bubble', 'panel'), may hold values from -6 to 6
- inv_diag: bfloat16 [128, 96, 128, 128], P('bubble', 'panel')
- near_vals: bfloat16 [128, 96, 4, 128, 128], P('bubble', 'panel'), may hold values from -0.25 to 0.25
- near_bubble: int32 [128, 96, 4], P('bubble', 'panel'), may hold values from 0 to 127, as said below
- near_block: int32 [128, 96, 4], P('bubble', 'panel'), may hold values from 0 to 95
- near_count: int32 [128, 96], P('bubble', 'panel'), may hold values from 1 to 4, as said below
- colour: int32 [128], P('bubble'), may hold values from 0 to 1
- moment_map: bfloat16 [128, 16, 12288], P('bubble', None, 'panel'), may hold values from -0.0546875 to 0.0546875
- spread_map: bfloat16 [128, 16, 12288], P('bubble', None, 'panel'), may hold values from -0.125 to 0.125
- centres: float32 [3, 128], replicated, may hold values from 0.2 to 6
Outputs:
- relaxed: float32 [128, 12288], P('bubble', 'panel')
Inputs may be any that keep to these rules, and one draw needn't show every extreme that they name: `near_bubble`: every slot of bubble b names a bubble within 8 of b. `near_count`: the first row block of every bubble uses all 4 slots.
All inputs are finite; a program needn't handle non-finite values.
Results may differ from a plain program's by a relative error of at most 0.0041.
Values may be sent and summed in bfloat16 or wider, within the bound.
No kernel may reach another device: no remote copies, remote signals or barrier semaphores. Data moves between devices by JAX's collectives and lax.ppermute only.
A program may use at most 64 MiB of HBM per device.

v0:
```python
import jax
import jax.numpy as jnp
from jax import lax
from jax.sharding import PartitionSpec as P


def with_halo(shard, sides, width):
    for axis, dim in sides:
        peers, length = (lax.axis_size(axis), shard.shape[dim])
        up = [(i, (i + 1) % peers) for i in range(peers - 1)]
        down = [(j, i) for i, j in up]
        last = lax.slice_in_dim(shard, length - width, length, axis=dim)
        first = lax.slice_in_dim(shard, 0, width, axis=dim)
        before = lax.ppermute(last, axis, up)
        after = lax.ppermute(first, axis, down)
        shard = jnp.concatenate([before, shard, after], axis=dim)
    return shard


def near_field(
    neighbourhood, near_vals, near_bubble, near_block, near_count, first_bubble, block_size
):
    rim_count = neighbourhood.shape[0]
    blocks = neighbourhood.reshape(rim_count, neighbourhood.shape[1] // block_size, block_size)
    local_bubble = near_bubble - first_bubble
    sources = blocks[local_bubble, near_block]
    live_slot = jnp.arange(near_vals.shape[2])[None, None, :] < near_count[:, :, None]
    sources = jnp.where(live_slot[:, :, :, None], sources, jnp.zeros_like(sources))
    return jnp.einsum("brsij,brsj->bri", near_vals, sources, preferred_element_type=jnp.float32)


def far_kernel(centres, my_bubbles, reach):
    centre_mine = centres[:, my_bubbles]
    diff = centre_mine[:, :, None] - centres[:, None, :]
    direct_sq = jnp.sum(diff * diff, axis=0)
    mirrored = centre_mine[2][:, None] + centres[2][None, :]
    image_sq = diff[0] * diff[0] + diff[1] * diff[1] + mirrored * mirrored
    kernel = 1.0 / jnp.sqrt(direct_sq + 1.0) + 1.0 / jnp.sqrt(image_sq + 1.0)
    gap = jnp.abs(my_bubbles[:, None] - jnp.arange(centres.shape[1])[None, :])
    return jnp.where(gap > reach, kernel, jnp.zeros_like(kernel))


def per_device(
    density,
    right_side,
    inv_diag,
    near_vals,
    near_bubble,
    near_block,
    near_count,
    colour,
    moment_map,
    spread_map,
    centres,
):
    bub_dev = density.shape[0]
    panels_dev = density.shape[1]
    block_size = inv_diag.shape[2]
    my_index = lax.axis_index("bubble")
    my_bubbles = my_index * bub_dev + jnp.arange(bub_dev, dtype=jnp.int32)
    first_bubble = my_index * bub_dev - bub_dev
    kernel = far_kernel(centres, my_bubbles, bub_dev)
    relaxed = density
    for colour_now in range(2):
        dens_bf = relaxed.astype(jnp.bfloat16)
        panel_full = lax.all_gather(dens_bf, "panel", axis=1, tiled=True)
        neighbourhood = with_halo(panel_full, (("bubble", 0),), bub_dev)
        near = near_field(
            neighbourhood, near_vals, near_bubble, near_block, near_count, first_bubble, block_size
        )
        partial_value = jnp.einsum(
            "bki,bi->bk", moment_map, dens_bf, preferred_element_type=jnp.float32
        )
        own_moments = lax.psum(partial_value, "panel")
        all_moments = lax.all_gather(own_moments, "bubble", axis=0, tiled=True)
        far_coeff = jnp.dot(kernel, all_moments, precision=lax.Precision.HIGHEST).astype(
            jnp.bfloat16
        )
        far = jnp.einsum("bki,bk->bi", spread_map, far_coeff, preferred_element_type=jnp.float32)
        remainder = (right_side - near.reshape(bub_dev, panels_dev) - far).astype(jnp.bfloat16)
        remainder = remainder.reshape(bub_dev, panels_dev // block_size, block_size)
        updated = jnp.einsum(
            "brij,brj->bri", inv_diag, remainder, preferred_element_type=jnp.float32
        )
        relaxed = jnp.where(
            (colour == colour_now)[:, None], updated.reshape(bub_dev, panels_dev), relaxed
        )
    return relaxed


def solution(mesh):
    in_specs = (
        P("bubble", "panel"),
        P("bubble", "panel"),
        P("bubble", "panel", None, None),
        P("bubble", "panel", None, None, None),
        P("bubble", "panel", None),
        P("bubble", "panel", None),
        P("bubble", "panel"),
        P("bubble"),
        P("bubble", None, "panel"),
        P("bubble", None, "panel"),
        P(),
    )
    out_specs = P("bubble", "panel")
    return jax.shard_map(
        per_device, mesh=mesh, in_specs=in_specs, out_specs=out_specs, check_vma=False
    )
```

profile of v0, /device:TPU:24, one launch (start us, length us, event | category | flops | bytes accessed | tf_op | source)
XLA Modules:
  0.0 213.0 jit_solution(4248419762880765899)
XLA Ops:
  0.0 0.9 convert_element_type.18
  0.9 19.4 %all_gather.12 = bf16[8,12288]{1,0:T(8,128)(2,1)S(1)} all-gather(bf16[8,768]{1,0:T(8,128)(2,1)S(1)} %convert_element_type.18), channel_id=1, replica_groups=mesh['bubble'=16,'panel'=16] {'panel'}, dimensions={1}, use_global_device_ids=true | all-gather | bytes 208896 | tf_op jit(solution)/shard_map/all_gather | solution.py:66
  20.2 3.8 %collective-permute-start = (bf16[8,12288]{1,0:T(8,128)(2,1)S(1)}, bf16[8,12288]{1,0:T(8,128)(2,1)S(1)}, u32[]{:S(2)}, u32[]{:S(2)}) collective-permute-start(bf16[8,12288]{1,0:T(8,128)(2,1)S(1)} %all_gather.12), channel_id=1, source_target_pairs={{0,16},{16,32},{32,48},{48,64},{64,80},{80,96},{96,112},{112,128},... | collective-permute-start | bytes 589832 | tf_op jit(solution)/shard_map/ppermute | solution.py:14
  24.0 6.2 %collective-permute-start.1 = (bf16[8,12288]{1,0:T(8,128)(2,1)S(1)}, bf16[8,12288]{1,0:T(8,128)(2,1)S(1)}, u32[]{:S(2)}, u32[]{:S(2)}) collective-permute-start(bf16[8,12288]{1,0:T(8,128)(2,1)S(1)} %all_gather.12), channel_id=1, source_target_pairs={{16,0},{32,16},{48,32},{64,48},{80,64},{96,80},{112,96},{128,112},... | collective-permute-start | bytes 589832 | tf_op jit(solution)/shard_map/ppermute | solution.py:15
  30.3 0.8 copy.18
  31.1 0.6 gather_fusion.1
  31.8 0.2 slice_reduce_fusion
  31.9 0.7 slice_bitcast_fusion
  32.6 0.7 convert_bitcast_fusion
  33.4 0.8 multiply_reduce_fusion
  34.1 1.1 fusion.16
  35.2 27.2 %psum.14 = f32[8,16]{1,0:T(8,128)S(1)} all-reduce(f32[8,16]{1,0:T(8,128)S(1)} %bitcast.107), channel_id=1, replica_groups=mesh['bubble'=16,'panel'=16] {'panel'}, use_global_device_ids=true, to_apply=%region_1.2 | all-reduce | flops 128 | bytes 1024 | tf_op jit(solution)/shard_map/psum | solution.py:74
  62.4 37.8 %all_gather.13 = f32[128,16]{1,0:T(8,128)S(1)} all-gather(f32[8,16]{1,0:T(8,128)S(1)} %psum.14), channel_id=1, replica_groups=mesh['bubble'=16,'panel'=16] {'bubble'}, dimensions={0}, use_global_device_ids=true | all-gather | bytes 8704 | tf_op jit(solution)/shard_map/all_gather | solution.py:75
  100.2 0.7 fusion.22
  101.2 0.8 iota_compare_fusion
  102.0 0.2 fusion
  102.2 1.1 fusion.34
  103.3 0.7 broadcast_compare_fusion.1
  104.1 2.5 %gather_fusion = bf16[192,128]{1,0:T(8,128)(2,1)S(1)} fusion(bf16[24,96,128]{2,1,0:T(8,128)(2,1)S(1)} %bitcast.101, s32[192]{0:T(256)S(1)} %reshape.62), kind=kCustom, calls=%fused_computation | custom fusion | bytes 99840 | tf_op jit(solution)/shard_map/gather | solution.py:26
  106.8 4.5 %fusion.4 = f32[8,6,1,128,1]{3,2,4,1,0:T(1,128)S(1)} fusion(bf16[8,6,4,128,128]{4,3,2,1,0:T(8,128)(2,1)} %param.14, bf16[8,6,4,128,1]{3,2,1,0,4:T(4,128)(2,1)S(1)} %select_bitcast_fusion.1), kind=kOutput, calls=%fused_computation.11 | convolution fusion | flops 6291456 | bytes 6365184 | tf_op jit(solution)/shard_map/brsij,brsj->bri/dot_general | solution.py:29
  111.3 0.9 fusion.14
  112.3 16.5 %all_gather.14 = bf16[8,12288]{1,0:T(8,128)(2,1)S(1)} all-gather(bf16[8,768]{1,0:T(8,128)(2,1)S(1)} %fusion.36), channel_id=1, replica_groups=mesh['bubble'=16,'panel'=16] {'panel'}, dimensions={1}, use_global_device_ids=true | all-gather | bytes 208896 | tf_op jit(solution)/shard_map/all_gather | solution.py:66
  128.8 2.0 collective-permute-start.2
  130.8 7.5 %collective-permute-start.3 = (bf16[8,12288]{1,0:T(8,128)(2,1)S(1)}, bf16[8,12288]{1,0:T(8,128)(2,1)S(1)}, u32[]{:S(2)}, u32[]{:S(2)}) collective-permute-start(bf16[8,12288]{1,0:T(8,128)(2,1)S(1)} %all_gather.14), channel_id=1, source_target_pairs={{16,0},{32,16},{48,32},{64,48},{80,64},{96,80},{112,96},{128,112},... | collective-permute-start | bytes 589832 | tf_op jit(solution)/shard_map/ppermute | solution.py:15
  138.4 28.5 %psum.15 = f32[8,16]{1,0:T(8,128)S(1)} all-reduce(f32[8,16]{1,0:T(8,128)S(1)} %bitcast.108), channel_id=1, replica_groups=mesh['bubble'=16,'panel'=16] {'panel'}, use_global_device_ids=true, to_apply=%region_2.3 | all-reduce | flops 128 | bytes 1024 | tf_op jit(solution)/shard_map/psum | solution.py:74
  166.9 36.7 %all_gather.15 = f32[128,16]{1,0:T(8,128)S(1)} all-gather(f32[8,16]{1,0:T(8,128)S(1)} %psum.15), channel_id=1, replica_groups=mesh['bubble'=16,'panel'=16] {'bubble'}, dimensions={0}, use_global_device_ids=true | all-gather | bytes 8704 | tf_op jit(solution)/shard_map/all_gather | solution.py:75
  203.7 0.2 fusion.1
  203.8 0.2 fusion.32
  204.2 2.5 %gather_fusion.2 = bf16[192,128]{1,0:T(8,128)(2,1)S(1)} fusion(bf16[24,96,128]{2,1,0:T(8,128)(2,1)S(1)} %bitcast.100, s32[192]{0:T(256)S(1)} %reshape.62), kind=kCustom, calls=%fused_computation.2 | custom fusion | bytes 99840 | tf_op jit(solution)/shard_map/gather | solution.py:26
  206.8 4.5 %fusion.2 = f32[8,6,1,128,1]{3,2,4,1,0:T(1,128)S(1)} fusion(bf16[8,6,4,128,128]{4,3,2,1,0:T(8,128)(2,1)} %param.14, bf16[8,6,4,128,1]{3,2,1,0,4:T(4,128)(2,1)S(1)} %select_bitcast_fusion), kind=kOutput, calls=%fused_computation.9 | convolution fusion | flops 6291456 | bytes 6365184 | tf_op jit(solution)/shard_map/brsij,brsj->bri/dot_general | solution.py:29
  211.3 0.9 fusion.10
  212.3 0.7 bitcast_select_fusion
  (31 shorter events, 1.2 us)
Async XLA Ops:
  0.0 111.3 %copy-start = (bf16[8,6,128,128]{3,2,1,0:T(8,128)(2,1)S(1)}, bf16[8,6,128,128]{3,2,1,0:T(8,128)(2,1)}, u32[]{:S(2)}) copy-start(bf16[8,6,128,128]{3,2,1,0:T(8,128)(2,1)} %param.13) | copy-start | bytes 4718596
  20.2 83.7 %collective-permute-start = (bf16[8,12288]{1,0:T(8,128)(2,1)S(1)}, bf16[8,12288]{1,0:T(8,128)(2,1)S(1)}, u32[]{:S(2)}, u32[]{:S(2)}) collective-permute-start(bf16[8,12288]{1,0:T(8,128)(2,1)S(1)} %all_gather.12), channel_id=1, source_target_pairs={{0,16},{16,32},{32,48},{48,64},{64,80},{80,96},{96,112},{112,128},... | collective-permute-start | bytes 589832 | tf_op jit(solution)/shard_map/ppermute | solution.py:14
  24.0 79.9 %collective-permute-start.1 = (bf16[8,12288]{1,0:T(8,128)(2,1)S(1)}, bf16[8,12288]{1,0:T(8,128)(2,1)S(1)}, u32[]{:S(2)}, u32[]{:S(2)}) collective-permute-start(bf16[8,12288]{1,0:T(8,128)(2,1)S(1)} %all_gather.12), channel_id=1, source_target_pairs={{16,0},{32,16},{48,32},{64,48},{80,64},{96,80},{112,96},{128,112},... | collective-permute-start | bytes 589832 | tf_op jit(solution)/shard_map/ppermute | solution.py:15
  106.7 4.5 %copy-start.3 = (f32[8,768]{1,0:T(8,128)S(1)}, f32[8,768]{1,0:T(8,128)}, u32[]{:S(2)}) copy-start(f32[8,768]{1,0:T(8,128)} %param.12) | copy-start | bytes 73732
  111.3 1.0 copy-start.2
  111.3 27.0 %copy-start.4 = (bf16[8,16,768]{2,1,0:T(8,128)(2,1)S(1)}, bf16[8,16,768]{2,1,0:T(8,128)(2,1)}, u32[]{:S(2)}) copy-start(bf16[8,16,768]{2,1,0:T(8,128)(2,1)} %param.19) | copy-start | bytes 589828
  111.3 92.5 %copy-start.1 = (bf16[8,16,768]{2,1,0:T(8,128)(2,1)S(1)}, bf16[8,16,768]{2,1,0:T(8,128)(2,1)}, u32[]{:S(2)}) copy-start(bf16[8,16,768]{2,1,0:T(8,128)(2,1)} %param.20) | copy-start | bytes 589828
  128.8 75.2 %collective-permute-start.2 = (bf16[8,12288]{1,0:T(8,128)(2,1)S(1)}, bf16[8,12288]{1,0:T(8,128)(2,1)S(1)}, u32[]{:S(2)}, u32[]{:S(2)}) collective-permute-start(bf16[8,12288]{1,0:T(8,128)(2,1)S(1)} %all_gather.14), channel_id=1, source_target_pairs={{0,16},{16,32},{32,48},{48,64},{64,80},{80,96},{96,112},{112,128},... | collective-permute-start | bytes 589832 | tf_op jit(solution)/shard_map/ppermute | solution.py:14
  130.8 73.2 %collective-permute-start.3 = (bf16[8,12288]{1,0:T(8,128)(2,1)S(1)}, bf16[8,12288]{1,0:T(8,128)(2,1)S(1)}, u32[]{:S(2)}, u32[]{:S(2)}) collective-permute-start(bf16[8,12288]{1,0:T(8,128)(2,1)S(1)} %all_gather.14), channel_id=1, source_target_pairs={{16,0},{32,16},{48,32},{64,48},{80,64},{96,80},{112,96},{128,112},... | collective-permute-start | bytes 589832 | tf_op jit(solution)/shard_map/ppermute | solution.py:15
where the time goes:
time: 214 us; the launch traced here: 213 us
  blocking collectives  166 us (78%)
  starting transfers between devices  19.5 us (9%)
  matrix products  13.6 us (6%)
  local copies, waits for them, and re-layouts  7.75 us (4%)
  other arithmetic  5.75 us (3%)
    all_gather x2, blocking collectives, per_device(): all_moments = lax.all_gather(own_moments, 'bubble', axis=0, tiled=True)  74.5 us
    psum x2, blocking collectives, per_device(): own_moments = lax.psum(partial_value, 'panel')  55.7 us
    all_gather x2, blocking collectives, per_device(): panel_full = lax.all_gather(dens_bf, 'panel', axis=1, tiled=True)  35.9 us
    ppermute x2, starting transfers between devices, with_halo(): after = lax.ppermute(first, axis, down)  13.7 us
    dot_general x2, matrix products, near_field(): jnp.einsum('brsij,brsj->bri', near_vals, sources, preferred_element_type=...  9.02 us
    ppermute x2, starting transfers between devices, with_halo(): before = lax.ppermute(last, axis, up)  5.78 us
    gather x2, local copies, waits for them, and re-layouts, near_field(): sources = blocks[local_bubble, near_block]  5.03 us
  transfers between devices with their start and end apart: 4, of which 0 were waited for; matrix products, arithmetic and copies ran while one was open for 4% of the time, Pallas kernels for 0%

commit v1 on v0

--- a/solution.py
+++ b/solution.py
@@ -72,7 +72,10 @@
             "bki,bi->bk", moment_map, dens_bf, preferred_element_type=jnp.float32
         )
         own_moments = lax.psum(partial_value, "panel")
-        all_moments = lax.all_gather(own_moments, "bubble", axis=0, tiled=True)
+        size = lax.axis_size("bubble")
+        parts = jnp.stack([own_moments for _ in range(size)])
+        parts = lax.all_to_all(parts, "bubble", split_axis=0, concat_axis=0)
+        all_moments = jnp.concatenate(parts, axis=0)
         far_coeff = jnp.dot(kernel, all_moments, precision=lax.Precision.HIGHEST).astype(
             jnp.bfloat16
         )

time: 214 us -> 164 us (0.77)
  blocking collectives: 166 us -> 90.2 us
  starting transfers between devices: 19.5 us -> 36 us
  waiting for transfers between devices: 0.01 us -> 4.73 us
  local copies, waits for them, and re-layouts: 7.75 us -> 9.9 us
    all_gather x2 -> x0, blocking collectives: 74.5 us -> none  [per_device(): all_moments = lax.all_gather(own_moments, 'bubble', axis=0, tiled=True)]
    all_to_all x0 -> x2, starting transfers between devices: none -> 16.5 us  [per_device(): parts = lax.all_to_all(parts, 'bubble', split_axis=0, concat_axis=0)]
  transfers between devices with their start and end apart: 4 -> 6, of which waited for: 0 -> 3; matrix products, arithmetic and copies ran while one was open for 4% -> 7% of each run, Pallas kernels for 0% -> 0%
where the time goes in v1:
time: 164 us; the launch traced here: 162 us
  blocking collectives  90.2 us (55%)
  starting transfers between devices  36 us (22%)
  matrix products  13.7 us (8%)
  local copies, waits for them, and re-layouts  9.9 us (6%)
  other arithmetic  7.18 us (4%)
  waiting for transfers between devices  4.73 us (3%)
    psum x2, blocking collectives, per_device(): own_moments = lax.psum(partial_value, 'panel')  54.3 us
    all_gather x2, blocking collectives, per_device(): panel_full = lax.all_gather(dens_bf, 'panel', axis=1, tiled=True)  35.8 us
    all_to_all x2, starting transfers between devices, per_device(): parts = lax.all_to_all(parts, 'bubble', split_axis=0, concat_axis=0)  16.5 us
    ppermute x2, starting transfers between devices, with_halo(): after = lax.ppermute(first, axis, down)  12.3 us
    dot_general x2, matrix products, near_field(): jnp.einsum('brsij,brsj->bri', near_vals, sources, preferred_element_type=...  9.02 us
    ppermute x2, starting transfers between devices, with_halo(): before = lax.ppermute(last, axis, up)  7.17 us
    gather x2, local copies, waits for them, and re-layouts, near_field(): sources = blocks[local_bubble, near_block]  5.03 us
  transfers between devices with their start and end apart: 6, of which 3 were waited for; matrix products, arithmetic and copies ran while one was open for 7% of the time, Pallas kernels for 0%

profile of v1, /device:TPU:24, one launch (start us, length us, event | category | flops | bytes accessed | tf_op | source)
XLA Modules:
  0.0 161.9 jit_solution(8193922411422380527)
XLA Ops:
  0.0 0.9 convert_element_type.18
  0.9 19.4 %all_gather.6 = bf16[8,12288]{1,0:T(8,128)(2,1)S(1)} all-gather(bf16[8,768]{1,0:T(8,128)(2,1)S(1)} %convert_element_type.18), channel_id=1, replica_groups=mesh['bubble'=16,'panel'=16] {'panel'}, dimensions={1}, use_global_device_ids=true | all-gather | bytes 208896 | tf_op jit(solution)/shard_map/all_gather | solution.py:66
  20.2 3.8 %collective-permute-start = (bf16[8,12288]{1,0:T(8,128)(2,1)S(1)}, bf16[8,12288]{1,0:T(8,128)(2,1)S(1)}, u32[]{:S(2)}, u32[]{:S(2)}) collective-permute-start(bf16[8,12288]{1,0:T(8,128)(2,1)S(1)} %all_gather.6), channel_id=1, source_target_pairs={{0,16},{16,32},{32,48},{48,64},{64,80},{80,96},{96,112},{112,128},... | collective-permute-start | bytes 589832 | tf_op jit(solution)/shard_map/ppermute | solution.py:14
  24.0 6.2 %collective-permute-start.1 = (bf16[8,12288]{1,0:T(8,128)(2,1)S(1)}, bf16[8,12288]{1,0:T(8,128)(2,1)S(1)}, u32[]{:S(2)}, u32[]{:S(2)}) collective-permute-start(bf16[8,12288]{1,0:T(8,128)(2,1)S(1)} %all_gather.6), channel_id=1, source_target_pairs={{16,0},{32,16},{48,32},{64,48},{80,64},{96,80},{112,96},{128,112},... | collective-permute-start | bytes 589832 | tf_op jit(solution)/shard_map/ppermute | solution.py:15
  30.3 0.7 convert_bitcast_fusion
  31.0 1.1 fusion.18
  32.1 27.2 %psum.14 = f32[8,16]{1,0:T(8,128)S(1)} all-reduce(f32[8,16]{1,0:T(8,128)S(1)} %bitcast.103), channel_id=1, replica_groups=mesh['bubble'=16,'panel'=16] {'panel'}, use_global_device_ids=true, to_apply=%region_1.2 | all-reduce | flops 128 | bytes 1024 | tf_op jit(solution)/shard_map/psum | solution.py:74
  59.3 0.7 reshape.248
  60.0 8.4 %all-to-all-start = ((f32[16,1,128]{2,1,0:T(1,128)}), f32[16,1,128]{2,1,0:T(1,128)S(1)}, u32[]{:S(2)}, u32[]{:S(2)}) async-start(f32[16,1,128]{2,1,0:T(1,128)} %reshape.248), calls=%async_computation | async-start | bytes 16384 | tf_op jit(solution)/shard_map/all_to_all | solution.py:77
  68.4 0.8 copy.18
  70.7 0.8 multiply_reduce_fusion
  71.5 0.8 iota_compare_fusion
  72.2 0.7 fusion.24
  74.0 1.5 all-to-all-done
  76.1 0.7 reduce.2
  77.0 1.1 fusion.36
  78.3 2.5 %gather_fusion = bf16[192,128]{1,0:T(8,128)(2,1)S(1)} fusion(bf16[24,96,128]{2,1,0:T(8,128)(2,1)S(1)} %bitcast.97, s32[192]{0:T(256)S(1)} %reshape.199), kind=kCustom, calls=%fused_computation | custom fusion | bytes 99840 | tf_op jit(solution)/shard_map/gather | solution.py:26
  80.9 4.5 %fusion.4 = f32[8,6,1,128,1]{3,2,4,1,0:T(1,128)S(1)} fusion(bf16[8,6,4,128,128]{4,3,2,1,0:T(8,128)(2,1)} %param.14, bf16[8,6,4,128,1]{3,2,1,0,4:T(4,128)(2,1)S(1)} %select_bitcast_fusion.1), kind=kOutput, calls=%fused_computation.11 | convolution fusion | flops 6291456 | bytes 6365184 | tf_op jit(solution)/shard_map/brsij,brsj->bri/dot_general | solution.py:29
  85.5 0.9 fusion.16
  86.7 27.1 %psum.15 = f32[8,16]{1,0:T(8,128)S(1)} all-reduce(f32[8,16]{1,0:T(8,128)S(1)} %bitcast.104), channel_id=1, replica_groups=mesh['bubble'=16,'panel'=16] {'panel'}, use_global_device_ids=true, to_apply=%region_2.3 | all-reduce | flops 128 | bytes 1024 | tf_op jit(solution)/shard_map/psum | solution.py:74
  113.8 0.7 reshape.250
  114.5 8.1 %all-to-all-start.1 = ((f32[16,1,128]{2,1,0:T(1,128)}), f32[16,1,128]{2,1,0:T(1,128)S(1)}, u32[]{:S(2)}, u32[]{:S(2)}) async-start(f32[16,1,128]{2,1,0:T(1,128)} %reshape.250), calls=%async_computation.1 | async-start | bytes 16384 | tf_op jit(solution)/shard_map/all_to_all | solution.py:77
  122.6 16.5 %all_gather.7 = bf16[8,12288]{1,0:T(8,128)(2,1)S(1)} all-gather(bf16[8,768]{1,0:T(8,128)(2,1)S(1)} %fusion.38), channel_id=1, replica_groups=mesh['bubble'=16,'panel'=16] {'panel'}, dimensions={1}, use_global_device_ids=true | all-gather | bytes 208896 | tf_op jit(solution)/shard_map/all_gather | solution.py:66
  139.1 3.4 %collective-permute-start.2 = (bf16[8,12288]{1,0:T(8,128)(2,1)S(1)}, bf16[8,12288]{1,0:T(8,128)(2,1)S(1)}, u32[]{:S(2)}, u32[]{:S(2)}) collective-permute-start(bf16[8,12288]{1,0:T(8,128)(2,1)S(1)} %all_gather.7), channel_id=1, source_target_pairs={{0,16},{16,32},{32,48},{48,64},{64,80},{80,96},{96,112},{112,128},... | collective-permute-start | bytes 589832 | tf_op jit(solution)/shard_map/ppermute | solution.py:14
  142.5 6.1 %collective-permute-start.3 = (bf16[8,12288]{1,0:T(8,128)(2,1)S(1)}, bf16[8,12288]{1,0:T(8,128)(2,1)S(1)}, u32[]{:S(2)}, u32[]{:S(2)}) collective-permute-start(bf16[8,12288]{1,0:T(8,128)(2,1)S(1)} %all_gather.7), channel_id=1, source_target_pairs={{16,0},{32,16},{48,32},{64,48},{80,64},{96,80},{112,96},{128,112},... | collective-permute-start | bytes 589832 | tf_op jit(solution)/shard_map/ppermute | solution.py:15
  148.6 0.7 reduce.3
  149.7 2.0 %collective-permute-done.2 = bf16[8,12288]{1,0:T(8,128)(2,1)S(1)} collective-permute-done((bf16[8,12288]{1,0:T(8,128)(2,1)S(1)}, bf16[8,12288]{1,0:T(8,128)(2,1)S(1)}, u32[]{:S(2)}, u32[]{:S(2)}) %collective-permute-start.2) | collective-permute-done | bytes 196640 | tf_op jit(solution)/shard_map/ppermute | solution.py:14
  151.8 1.2 collective-permute-done.3
  153.1 2.5 %gather_fusion.2 = bf16[192,128]{1,0:T(8,128)(2,1)S(1)} fusion(bf16[24,96,128]{2,1,0:T(8,128)(2,1)S(1)} %bitcast.96, s32[192]{0:T(256)S(1)} %reshape.199), kind=kCustom, calls=%fused_computation.2 | custom fusion | bytes 99840 | tf_op jit(solution)/shard_map/gather | solution.py:26
  155.7 4.5 %fusion.2 = f32[8,6,1,128,1]{3,2,4,1,0:T(1,128)S(1)} fusion(bf16[8,6,4,128,128]{4,3,2,1,0:T(8,128)(2,1)} %param.14, bf16[8,6,4,128,1]{3,2,1,0,4:T(4,128)(2,1)S(1)} %select_bitcast_fusion), kind=kOutput, calls=%fused_computation.9 | convolution fusion | flops 6291456 | bytes 6365184 | tf_op jit(solution)/shard_map/brsij,brsj->bri/dot_general | solution.py:29
  160.3 0.9 fusion.12
  161.2 0.7 bitcast_select_fusion
  (42 shorter events, 4.5 us)
Async XLA Ops:
  0.0 85.5 %copy-start = (bf16[8,6,128,128]{3,2,1,0:T(8,128)(2,1)S(1)}, bf16[8,6,128,128]{3,2,1,0:T(8,128)(2,1)}, u32[]{:S(2)}) copy-start(bf16[8,6,128,128]{3,2,1,0:T(8,128)(2,1)} %param.13) | copy-start | bytes 4718596
  20.2 57.9 %collective-permute-start = (bf16[8,12288]{1,0:T(8,128)(2,1)S(1)}, bf16[8,12288]{1,0:T(8,128)(2,1)S(1)}, u32[]{:S(2)}, u32[]{:S(2)}) collective-permute-start(bf16[8,12288]{1,0:T(8,128)(2,1)S(1)} %all_gather.6), channel_id=1, source_target_pairs={{0,16},{16,32},{32,48},{48,64},{64,80},{80,96},{96,112},{112,128},... | collective-permute-start | bytes 589832 | tf_op jit(solution)/shard_map/ppermute | solution.py:14
  24.0 54.1 %collective-permute-start.1 = (bf16[8,12288]{1,0:T(8,128)(2,1)S(1)}, bf16[8,12288]{1,0:T(8,128)(2,1)S(1)}, u32[]{:S(2)}, u32[]{:S(2)}) collective-permute-start(bf16[8,12288]{1,0:T(8,128)(2,1)S(1)} %all_gather.6), channel_id=1, source_target_pairs={{16,0},{32,16},{48,32},{64,48},{80,64},{96,80},{112,96},{128,112},... | collective-permute-start | bytes 589832 | tf_op jit(solution)/shard_map/ppermute | solution.py:15
  60.0 15.5 %all-to-all-start = ((f32[16,1,128]{2,1,0:T(1,128)}), f32[16,1,128]{2,1,0:T(1,128)S(1)}, u32[]{:S(2)}, u32[]{:S(2)}) async-start(f32[16,1,128]{2,1,0:T(1,128)} %reshape.248), calls=%async_computation | async-start | bytes 16384 | tf_op jit(solution)/shard_map/all_to_all | solution.py:77
  80.9 4.5 %copy-start.3 = (f32[8,768]{1,0:T(8,128)S(1)}, f32[8,768]{1,0:T(8,128)}, u32[]{:S(2)}) copy-start(f32[8,768]{1,0:T(8,128)} %param.12) | copy-start | bytes 73732
  85.4 1.0 copy-start.2
  85.4 1.0 copy-start.4
  85.4 64.1 %copy-start.1 = (bf16[8,16,768]{2,1,0:T(8,128)(2,1)S(1)}, bf16[8,16,768]{2,1,0:T(8,128)(2,1)}, u32[]{:S(2)}) copy-start(bf16[8,16,768]{2,1,0:T(8,128)(2,1)} %param.20) | copy-start | bytes 589828
  114.5 34.1 %all-to-all-start.1 = ((f32[16,1,128]{2,1,0:T(1,128)}), f32[16,1,128]{2,1,0:T(1,128)S(1)}, u32[]{:S(2)}, u32[]{:S(2)}) async-start(f32[16,1,128]{2,1,0:T(1,128)} %reshape.250), calls=%async_computation.1 | async-start | bytes 16384 | tf_op jit(solution)/shard_map/all_to_all | solution.py:77
  139.1 12.6 %collective-permute-start.2 = (bf16[8,12288]{1,0:T(8,128)(2,1)S(1)}, bf16[8,12288]{1,0:T(8,128)(2,1)S(1)}, u32[]{:S(2)}, u32[]{:S(2)}) collective-permute-start(bf16[8,12288]{1,0:T(8,128)(2,1)S(1)} %all_gather.7), channel_id=1, source_target_pairs={{0,16},{16,32},{32,48},{48,64},{64,80},{80,96},{96,112},{112,128},... | collective-permute-start | bytes 589832 | tf_op jit(solution)/shard_map/ppermute | solution.py:14
  142.5 10.5 %collective-permute-start.3 = (bf16[8,12288]{1,0:T(8,128)(2,1)S(1)}, bf16[8,12288]{1,0:T(8,128)(2,1)S(1)}, u32[]{:S(2)}, u32[]{:S(2)}) collective-permute-start(bf16[8,12288]{1,0:T(8,128)(2,1)S(1)} %all_gather.7), channel_id=1, source_target_pairs={{16,0},{32,16},{48,32},{64,48},{80,64},{96,80},{112,96},{128,112},... | collective-permute-start | bytes 589832 | tf_op jit(solution)/shard_map/ppermute | solution.py:15
